TPU v7x, 128 devices: a whole 4x4x4 slice. The times are simulated.
128 devices in a mesh: dp: 8 (over y, core), expert: 16 (over z, x).
Axes of the slice: x: 4, y: 4, z: 4, core: 2. Of those that a mesh axis runs over, the one named last changes fastest.
Arguments:
- tokens: bfloat16 [16384, 4096], P(('dp', 'expert')), may hold values from -6 to 6
- router_weights: float32 [16384, 8], P(('dp', 'expert')), may hold values from 0.1 to 1
- expert_ids: int32 [16384, 8], P(('dp', 'expert')), may hold values from 0 to 127, as said below
- gate_weight: bfloat16 [128, 4096, 768], P(('dp', 'expert')), may hold values from -0.09375 to 0.09375
- up_weight: bfloat16 [128, 4096, 768], P(('dp', 'expert')), may hold values from -0.09375 to 0.09375
- down_weight: bfloat16 [128, 768, 4096], P(('dp', 'expert')), may hold values from -0.21875 to 0.21875
Outputs:
- mixed: bfloat16 [16384, 4096], P(('dp', 'expert'))
Inputs may be any that keep to these rules, and one draw needn't show every extreme that they name: `expert_ids`: each row names 8 different experts. Experts e and e + 16 with e // 16 even form a pair: the 128 tokens of one device (aligned blocks of rows) name the two experts of each pair exactly 2 * 8 times together, and one expert at most 12 times; some expert is named exactly 12 times by the tokens of every device.
All inputs are finite; a program needn't handle non-finite values.
Results may differ from a plain program's by a relative error of at most 0.0058.
Values may be sent and summed in bfloat16 or wider, within the bound.
A program may use at most 192 MiB of HBM per device.

v0:
```python
import jax
import jax.numpy as jnp
from jax import lax
from jax.sharding import PartitionSpec as P


def expert_apply(row_block, w_gate, w_up, w_down):
    gate_proj = jnp.dot(row_block, w_gate, preferred_element_type=jnp.float32)
    up_proj = jnp.dot(row_block, w_up, preferred_element_type=jnp.float32)
    hidden = (jax.nn.silu(gate_proj) * up_proj).astype(jnp.bfloat16)
    return jnp.dot(hidden, w_down, preferred_element_type=jnp.float32).astype(jnp.bfloat16)


def inverse_of(ordering):
    entries = ordering.shape[0]
    return jnp.zeros((entries,), jnp.int32).at[ordering].set(jnp.arange(entries, dtype=jnp.int32))


def local(tokens, router_weights, expert_ids, gate_weight, up_weight, down_weight):
    lane_count = lax.axis_size("expert")
    group_count = lax.axis_size("dp")
    experts = group_count * lane_count
    choices_per = expert_ids.shape[1]
    model_width = tokens.shape[1]
    assign_total = expert_ids.size
    slot_cap = assign_total // experts
    block_rows = 128
    flat_ids = expert_ids.reshape(-1)
    one_hot = (flat_ids[:, None] == jnp.arange(experts, dtype=jnp.int32)[None, :]).astype(jnp.int32)
    position = jnp.sum((jnp.cumsum(one_hot, axis=0) - one_hot) * one_hot, axis=1)
    w_gate = gate_weight[0]
    w_up = up_weight[0]
    w_down = down_weight[0]
    slot_most = 3 * slot_cap // 2
    slot_total = experts * slot_most
    target = flat_ids * slot_most + position
    anchor = (
        jnp.zeros((slot_total,), jnp.int32)
        .at[target]
        .set(jnp.arange(assign_total, dtype=jnp.int32))
    )
    filled = jnp.zeros((slot_total,), jnp.bfloat16).at[target].set(1.0)
    send_rows = tokens[anchor // choices_per]
    arrived, markers = (
        lax.all_to_all(
            send_rows.reshape(experts, slot_most, model_width),
            ("dp", "expert"),
            split_axis=0,
            concat_axis=0,
            tiled=True,
        ),
        lax.all_to_all(
            filled.reshape(experts, slot_most),
            ("dp", "expert"),
            split_axis=0,
            concat_axis=0,
            tiled=True,
        ),
    )
    arrived = arrived.reshape(slot_total, model_width)
    is_valid = (markers.reshape(-1) > 0.5).astype(jnp.int32)
    ordering = jnp.argsort(1 - is_valid, stable=True)
    valid_count = jnp.sum(is_valid)
    sorted_rows = arrived[ordering]
    blocks_used = (valid_count + block_rows - 1) // block_rows

    def compute(step_index, written):
        offset = step_index * block_rows
        row_block = lax.dynamic_slice_in_dim(sorted_rows, offset, block_rows)
        return lax.dynamic_update_slice_in_dim(
            written, expert_apply(row_block, w_gate, w_up, w_down), offset, 0
        )

    finished = lax.fori_loop(
        0, blocks_used, compute, jnp.zeros((slot_total, model_width), jnp.bfloat16)
    )
    results = finished[inverse_of(ordering)]
    returned = lax.all_to_all(
        results.reshape(experts, slot_most, model_width),
        ("dp", "expert"),
        split_axis=0,
        concat_axis=0,
        tiled=True,
    )
    returned = returned.reshape(-1, model_width)[target]
    combined = jnp.sum(
        router_weights[:, :, None]
        * returned.reshape(-1, choices_per, model_width).astype(jnp.float32),
        axis=1,
    )
    return combined.astype(jnp.bfloat16)


def solution(mesh):
    return jax.shard_map(
        local,
        mesh=mesh,
        in_specs=(
            P(("dp", "expert"), None),
            P(("dp", "expert"), None),
            P(("dp", "expert"), None),
            P(("dp", "expert"), None, None),
            P(("dp", "expert"), None, None),
            P(("dp", "expert"), None, None),
        ),
        out_specs=P(("dp", "expert"), None),
        check_vma=False,
    )
```

profile of v0, /device:TPU:5, one launch (start us, length us, event | category | flops | bytes accessed | tf_op | source)
XLA Modules:
  0.0 856.6 jit_solution(16922940872511186691)
XLA Ops:
  0.0 0.9 copy.16
  1.1 0.7 broadcast_multiply_fusion
  1.8 0.1 copy.18
  1.9 0.2 fusion.20
  2.1 0.1 copy.19
  2.3 0.1 copy.15
  2.4 0.1 mul.40
  2.5 0.4 fusion.19
  2.9 7.6 scatter_custom_fusion
  10.5 0.8 all_to_all.16
  11.2 10.8 %all-to-all-start = ((bf16[128,1,12]{2,1,0:T(2,128)(2,1)}), bf16[128,1,12]{2,1,0:T(2,128)(2,1)S(1)}, u32[]{:S(2)}, u32[]{:S(2)}) async-start(bf16[128,1,12]{2,1,0:T(2,128)(2,1)} %all_to_all.16), calls=%async_computation | async-start | bytes 131072 | tf_op jit(solution)/shard_map/all_to_all | solution.py:52
  22.1 4.3 scatter_custom_fusion.1
  26.4 9.5 %gather_fusion = bf16[1536,4096]{1,0:T(8,128)(2,1)} fusion(bf16[128,4096]{1,0:T(8,128)(2,1)S(1)} %copy-done, s32[2048]{0:T(1024)S(1)} %pad_clamp_fusion.2), kind=kCustom, calls=%fused_computation | custom fusion | bytes 25171968 | tf_op jit(solution)/shard_map/gather | solution.py:43
  36.0 17.9 %reshape.77 = bf16[128,12,4096]{2,1,0:T(8,128)(2,1)} reshape(bf16[1536,4096]{1,0:T(8,128)(2,1)} %gather_fusion) | data formatting | bytes 25165824 | tf_op jit(solution)/shard_map/reshape | solution.py:46
  53.9 10.2 %all-to-all-start.1 = ((bf16[128,12,4096]{2,1,0:T(8,128)(2,1)}), bf16[128,12,4096]{2,1,0:T(8,128)(2,1)}, u32[]{:S(2)}, u32[]{:S(2)}) async-start(bf16[128,12,4096]{2,1,0:T(8,128)(2,1)} %reshape.77), calls=%async_computation.1 | async-start | bytes 33554432 | tf_op jit(solution)/shard_map/all_to_all | solution.py:45
  64.1 0.9 subtract_reduce_fusion
  65.7 0.1 sub.28
  65.8 5.0 sort.17
  70.8 6.6 scatter_custom_fusion.2
  77.5 234.2 %all-to-all-done.1 = bf16[128,12,4096]{2,1,0:T(8,128)(2,1)} async-done(((bf16[128,12,4096]{2,1,0:T(8,128)(2,1)}), bf16[128,12,4096]{2,1,0:T(8,128)(2,1)}, u32[]{:S(2)}, u32[]{:S(2)}) %all-to-all-start.1) | async-done | bytes 12582944 | tf_op jit(solution)/shard_map/all_to_all | solution.py:45
  311.7 18.2 %reshape.78 = bf16[1536,4096]{1,0:T(8,128)(2,1)} reshape(bf16[128,12,4096]{2,1,0:T(8,128)(2,1)} %all-to-all-done.1) | data formatting | bytes 25165824 | tf_op jit(solution)/shard_map/reshape | solution.py:60
  329.9 28.2 %gather_fusion.1 = bf16[1536,4096]{1,0:T(8,128)(2,1)} fusion(bf16[1536,4096]{1,0:T(8,128)(2,1)} %reshape.78, s32[2048]{0:T(1024)S(1)} %pad_clamp_fusion.1), kind=kCustom, calls=%fused_computation.1 | custom fusion | bytes 25171968 | tf_op jit(solution)/shard_map/gather | solution.py:64
  358.1 6.1 broadcast_in_dim.24
  364.2 100.0 %while.10 = (s32[]{:T(128)}, bf16[1536,4096]{1,0:T(8,128)(2,1)}, s32[]{:T(128)}, bf16[1536,4096]{1,0:T(8,128)(2,1)}, bf16[4096,768]{1,0:T(8,128)(2,1)}, /*index=...) while((s32[]{:T(128)}, bf16[1536,4096]{1,0:T(8,128)(2,1)}, ...), condition=%wide.region_8.9_spmd, body=%wide.region_7.8_spmd.sunk | while | flops 2417033216 | bytes 22807712 | solution.py:74
  364.2 4.1 fusion.47
  368.3 8.4 fusion.48
  376.7 4.1 fusion.47
  380.8 8.3 fusion.48
  389.1 4.1 fusion.47
  393.2 8.3 fusion.48
  401.6 4.1 fusion.47
  405.7 8.4 fusion.48
  414.1 4.1 fusion.47
  418.2 8.4 fusion.48
  426.5 4.1 fusion.47
  430.6 8.4 fusion.48
  439.0 4.1 fusion.47
  443.2 8.4 fusion.48
  451.5 4.1 fusion.47
  455.6 8.4 fusion.48
  464.1 28.2 %gather_fusion.2 = bf16[1536,4096]{1,0:T(8,128)(2,1)} fusion(bf16[1536,4096]{1,0:T(8,128)(2,1)} %get-tuple-element.45, s32[2048]{0:T(1024)S(1)} %pad_clamp_fusion), kind=kCustom, calls=%fused_computation.2 | custom fusion | bytes 25171968 | tf_op jit(solution)/shard_map/gather | solution.py:77
  492.4 17.9 %reshape.79 = bf16[128,12,4096]{2,1,0:T(8,128)(2,1)} reshape(bf16[1536,4096]{1,0:T(8,128)(2,1)} %gather_fusion.2) | data formatting | bytes 25165824 | tf_op jit(solution)/shard_map/reshape | solution.py:79
  510.2 45.9 %all-to-all-start.2 = ((bf16[128,12,4096]{2,1,0:T(8,128)(2,1)}), bf16[128,12,4096]{2,1,0:T(8,128)(2,1)}, u32[]{:S(2)}, u32[]{:S(2)}) async-start(bf16[128,12,4096]{2,1,0:T(8,128)(2,1)} %reshape.79), calls=%async_computation.2 | async-start | bytes 33554432 | tf_op jit(solution)/shard_map/all_to_all | solution.py:78
  556.2 0.1 copy.14
  556.3 247.5 %all-to-all-done.2 = bf16[128,12,4096]{2,1,0:T(8,128)(2,1)} async-done(((bf16[128,12,4096]{2,1,0:T(8,128)(2,1)}), bf16[128,12,4096]{2,1,0:T(8,128)(2,1)}, u32[]{:S(2)}, u32[]{:S(2)}) %all-to-all-start.2) | async-done | bytes 12582944 | tf_op jit(solution)/shard_map/all_to_all | solution.py:78
  803.8 18.2 %reshape.80 = bf16[1536,4096]{1,0:T(8,128)(2,1)} reshape(bf16[128,12,4096]{2,1,0:T(8,128)(2,1)} %all-to-all-done.2) | data formatting | bytes 25165824 | tf_op jit(solution)/shard_map/reshape | solution.py:85
  821.9 21.5 %gather_fusion.3 = bf16[1024,4096]{1,0:T(8,128)(2,1)} fusion(bf16[1536,4096]{1,0:T(8,128)(2,1)} %reshape.80, s32[1024]{0:T(1024)S(1)} %broadcast_clamp_fusion), kind=kCustom, calls=%fused_computation.3 | custom fusion | bytes 16781312 | tf_op jit(solution)/shard_map/gather | solution.py:85
  843.5 12.9 %fusion.17 = bf16[128,4096]{1,0:T(8,128)(2,1)} fusion(bf16[1024,4096]{1,0:T(8,128)(2,1)} %gather_fusion.3, f32[128,8]{1,0:T(8,128)S(1)} %copy.14), kind=kLoop, calls=%fused_computation.24 | loop fusion | flops 12058624 | bytes 9441280 | tf_op jit(solution)/shard_map/reduce_sum | solution.py:86
  (29 shorter events, 0.3 us)
Async XLA Ops:
  0.0 26.4 %copy-start = (bf16[128,4096]{1,0:T(8,128)(2,1)S(1)}, bf16[128,4096]{1,0:T(8,128)(2,1)}, u32[]{:S(2)}) copy-start(bf16[128,4096]{1,0:T(8,128)(2,1)} %param.8) | copy-start | bytes 3145732
  2.8 33.1 %copy-start.2 = (s32[1024,1]{0,1:T(1,128)}, s32[1024,1]{0,1:T(1,128)S(1)}, u32[]{:S(2)}) copy-start(s32[1024,1]{0,1:T(1,128)S(1)} %compare_select_fusion) | copy-start | bytes 12292
  11.2 42.6 %all-to-all-start = ((bf16[128,1,12]{2,1,0:T(2,128)(2,1)}), bf16[128,1,12]{2,1,0:T(2,128)(2,1)S(1)}, u32[]{:S(2)}, u32[]{:S(2)}) async-start(bf16[128,1,12]{2,1,0:T(2,128)(2,1)} %all_to_all.16), calls=%async_computation | async-start | bytes 131072 | tf_op jit(solution)/shard_map/all_to_all | solution.py:52
  53.9 257.8 %all-to-all-start.1 = ((bf16[128,12,4096]{2,1,0:T(8,128)(2,1)}), bf16[128,12,4096]{2,1,0:T(8,128)(2,1)}, u32[]{:S(2)}, u32[]{:S(2)}) async-start(bf16[128,12,4096]{2,1,0:T(8,128)(2,1)} %reshape.77), calls=%async_computation.1 | async-start | bytes 33554432 | tf_op jit(solution)/shard_map/all_to_all | solution.py:45
  510.2 45.9 %copy-start.4 = (f32[128,8]{0,1:T(8,128)S(1)}, f32[128,8]{0,1:T(8,128)}, u32[]{:S(2)}) copy-start(f32[128,8]{0,1:T(8,128)} %param.9) | copy-start | bytes 12292
  510.2 46.0 %copy-start.3 = (s32[1024,1]{0,1:T(1,128)S(1)}, s32[1024,1]{0,1:T(1,128)}, u32[]{:S(2)}) copy-start(s32[1024,1]{0,1:T(1,128)} %copy-done.2) | copy-start | bytes 12292
  510.2 293.5 %all-to-all-start.2 = ((bf16[128,12,4096]{2,1,0:T(8,128)(2,1)}), bf16[128,12,4096]{2,1,0:T(8,128)(2,1)}, u32[]{:S(2)}, u32[]{:S(2)}) async-start(bf16[128,12,4096]{2,1,0:T(8,128)(2,1)} %reshape.79), calls=%async_computation.2 | async-start | bytes 33554432 | tf_op jit(solution)/shard_map/all_to_all | solution.py:78
  821.9 34.4 %copy-start.1 = (bf16[128,4096]{1,0:T(8,128)(2,1)S(1)}, bf16[128,4096]{1,0:T(8,128)(2,1)}, u32[]{:S(2)}) copy-start(bf16[128,4096]{1,0:T(8,128)(2,1)} %param.8) | copy-start | bytes 3145732
where the time goes:
time: 867 us; the launch traced here: 857 us
  waiting for transfers between devices  482 us (56%)
  local copies, waits for them, and re-layouts  187 us (22%)
  matrix products  99.7 us (11%)
  starting transfers between devices  66.9 us (8%)
  other arithmetic  20.2 us (2%)
    all_to_all x1, waiting for transfers between devices, local(): lax.all_to_all(results.reshape(experts, slot_most, model_width), ('dp', '...  247 us
    all_to_all x1, waiting for transfers between devices, local(): lax.all_to_all(send_rows.reshape(experts, slot_most, model_width), ('dp',...  234 us
    dot_general x8, matrix products, expert_apply(): jnp.dot(hidden, w_down, preferred_element_type=jnp.float32)  66.9 us
    all_to_all x1, starting transfers between devices, local(): lax.all_to_all(results.reshape(experts, slot_most, model_width), ('dp', '...  45.9 us
    dot_general x8, matrix products, expert_apply(): gate_proj = jnp.dot(row_block, w_gate, preferred_element_type=jnp.float32)  32.8 us
    gather x1, local copies, waits for them, and re-layouts, local(): results = finished[inverse_of(ordering)]  28.2 us
    gather x1, local copies, waits for them, and re-layouts, local(): sorted_rows = arrived[ordering]  28.2 us
    gather x1, local copies, waits for them, and re-layouts, local(): returned = returned.reshape(-1, model_width)[target]  21.5 us
  transfers between devices with their start and end apart: 3, of which 2 were waited for; matrix products, arithmetic and copies ran while one was open for 5% of the time, Pallas kernels for 0%

commit v1 on v0

v1 whole, which is shorter than its diff:
```python
import jax
import jax.numpy as jnp
import itertools
from jax import lax
from jax.experimental import pallas as pl
from jax.experimental.pallas import tpu as pltpu
from jax.sharding import PartitionSpec as P

MESH = pl.DeviceIdType.MESH
F32 = jnp.float32
BF16 = jnp.bfloat16
D = 4096
FF = 768
CHIPS = 64
GS = 16
NG = CHIPS // GS
CT = 512
NT = D // CT


def balanced_order():
    every = list(itertools.product(range(4), repeat=3))
    left = set(every[1:])
    order = [every[0]]
    kinds = sorted(itertools.product(range(3), repeat=3), key=lambda t: (-t.count(1), t))
    for kind in kinds:
        ones = [i for i in range(3) if kind[i] == 1]
        twin = tuple(2 - d for d in kind)
        for signs in itertools.product((1, 3), repeat=len(ones)):
            flipped = tuple(4 - s for s in signs)
            for base, sg in ((kind, signs), (twin, flipped), (kind, flipped), (twin, signs)):
                offset = list(base)
                for i, s in zip(ones, sg):
                    offset[i] = s
                offset = tuple(offset)
                if offset in left:
                    left.remove(offset)
                    order.append(offset)
    return order


ORDER = balanced_order()
WORDS = [
    [sum(ORDER[8 * b + j][axis] * 4**j for j in range(8)) for b in range(8)] for axis in range(3)
]


def pick_word(b, words):
    value = jnp.int32(words[0])
    for k in range(1, 8):
        value = jnp.where(b == k, jnp.int32(words[k]), value)
    return value


def offsets_of(b):
    found = [pick_word(b, WORDS[axis]) for axis in range(3)]
    return [tuple(lax.rem(lax.div(w, jnp.int32(4**j)), jnp.int32(4)) for w in found) for j in range(8)]


def kernel(
    tok_hbm, ids_ref, rw_ref, wg_hbm, wu_hbm, wd_hbm,
    out_ref,
    tok, aux, auxs, cnt, meta, onehot, send, arr, pmix, pout, ret,
    wg, wu, wd, xs, hid, comb, acc, part,
    in_sem, wt_sem, start_s, start_r, meta_s, meta_r, disp_s, disp_r, ret_s, ret_r,
    mix_s, mix_r, po_s, po_r, part_s, part_r,
):
    dp = lax.axis_index("dp")
    ex = lax.axis_index("expert")
    y, c = dp // 2, dp % 2
    z, x = ex // 4, ex % 4
    partner = (y * 2 + (1 - c), ex)

    def chip_at(o, sign):
        dx, dy, dz = o
        xx = lax.rem(x + (dx if sign > 0 else 4 - dx), 4)
        yy = lax.rem(y + (dy if sign > 0 else 4 - dy), 4)
        zz = lax.rem(z + (dz if sign > 0 else 4 - dz), 4)
        return xx, yy, zz

    def device_at(o, sign):
        xx, yy, zz = chip_at(o, sign)
        return (yy * 2 + c, zz * 4 + xx)

    def pair_at(o):
        xx, yy, zz = chip_at(o, 1)
        return yy * 16 + zz * 4 + xx

    tok_in = pltpu.make_async_copy(tok_hbm, tok.at[c], in_sem)
    tok_in.start()
    w_in = [
        pltpu.make_async_copy(src, dst, wt_sem.at[i])
        for i, (src, dst) in enumerate(((wg_hbm, wg), (wu_hbm, wu), (wd_hbm, wd)))
    ]
    for copy in w_in:
        copy.start()

    barrier = pltpu.get_barrier_semaphore()
    pl.semaphore_signal(barrier, inc=1, device_id=partner, device_id_type=MESH)

    def greet(i, carry):
        other = device_at((i // 16, (i // 4) % 4, i % 4), 1)
        pl.semaphore_signal(barrier, inc=1, device_id=other, device_id_type=MESH)
        return carry

    lax.fori_loop(1, CHIPS, greet, 0)

    expert_io = lax.broadcasted_iota(jnp.int32, (128, 128), 0)
    named = jnp.zeros((128, 128), F32)
    weight = jnp.zeros((128, 128), F32)
    for k in range(8):
        hit = expert_io == ids_ref[k : k + 1, :]
        named = named + jnp.where(hit, 1.0, 0.0)
        weight = weight + jnp.where(hit, rw_ref[k : k + 1, :], 0.0)
    t_from = lax.broadcasted_iota(jnp.int32, (128, 128), 0)
    t_to = lax.broadcasted_iota(jnp.int32, (128, 128), 1)
    before = jnp.where(t_from < t_to, 1.0, 0.0).astype(BF16)
    rank = jnp.dot(named.astype(BF16), before, preferred_element_type=F32)
    counts = lax.dot_general(
        jnp.ones((8, 128), BF16), named.astype(BF16), (((1,), (1,)), ((), ())),
        preferred_element_type=F32,
    )

    def side(values, low):
        return jnp.concatenate(
            [values[32 * k + 16 * low : 32 * k + 16 * low + 16] for k in range(4)], axis=0
        )

    named2 = [side(named, 0), side(named, 1)]
    weight2 = [side(weight, 0), side(weight, 1)]
    rank2 = [side(rank, 0), side(rank, 1)]
    shift = (4 * c).astype(F32)

    def view(own, other):
        q_own = rank2[own]
        row_own = jnp.where(
            (named2[own] > 0.5) & (q_own < 7.5), q_own + jnp.where(q_own > 3.5, 4.0, 0.0) + shift, -1.0
        )
        q_other = 15.0 - rank2[other]
        row_other = jnp.where((named2[other] > 0.5) & (q_other < 7.5), q_other + 4.0 + shift, -1.0)
        return row_own, row_other, weight2[own], weight2[other]

    views = (view(0, 1), view(1, 0))
    for k in range(4):
        aux[c, k] = jnp.where(c == 0, views[0][k], views[1][k])
        auxs[k] = jnp.where(c == 0, views[1][k], views[0][k])
    cnt[c] = counts[0:1, :]

    pl.semaphore_wait(barrier, CHIPS)

    starts = [
        pltpu.make_async_remote_copy(
            src, dst, start_s.at[i], start_r.at[i], device_id=partner, device_id_type=MESH
        )
        for i, (src, dst) in enumerate(
            ((auxs, aux.at[c]), (cnt.at[c], cnt.at[c]), (tok_hbm, tok.at[c]))
        )
    ]
    for copy in starts:
        copy.start()
    tok_in.wait()
    for copy in starts:
        copy.wait()

    meta[0] = cnt[...]

    def meta_copy(i, o):
        return pltpu.make_async_remote_copy(
            cnt, meta.at[i], meta_s.at[i], meta_r.at[i],
            device_id=device_at(o, 1), device_id_type=MESH,
        )

    def send_copy(i, o):
        return pltpu.make_async_remote_copy(
            send.at[i], arr.at[i], disp_s.at[i], disp_r.at[i],
            device_id=device_at(o, 1), device_id_type=MESH,
        )

    def ret_copy(i, o):
        return pltpu.make_async_remote_copy(
            arr.at[i], ret.at[i], ret_s.at[i], ret_r.at[i],
            device_id=device_at(o, -1), device_id_type=MESH,
        )

    row_io = lax.broadcasted_iota(jnp.int32, (16, 256), 0).astype(F32)

    def aux_row(k, pair):
        return jnp.concatenate(
            [aux[0, k, pl.ds(pair, 1), :], aux[1, k, pl.ds(pair, 1), :]], axis=1
        )

    def dispatch(b, carry):
        offs = offsets_of(b)
        for j in range(8):
            pair = pair_at(offs[j])
            hit = (row_io == aux_row(0, pair)) | (row_io == aux_row(1, pair))
            onehot[16 * j : 16 * j + 16, :] = jnp.where(hit, 1.0, 0.0).astype(BF16)

        def tile(n, inner):
            cols = pl.ds(pl.multiple_of(n * CT, CT), CT)
            rows = jnp.dot(
                onehot[...], tok[:, :, cols].reshape(256, CT), preferred_element_type=F32
            )
            send[pl.ds(b * 8, 8), :, :, cols] = rows.reshape(8, 2, 8, CT).astype(BF16)
            return inner

        lax.fori_loop(0, NT, tile, 0)
        for j in range(8):
            i = b * 8 + j

            def go(i=i, j=j):
                meta_copy(i, offs[j]).start()
                send_copy(i, offs[j]).start()

            if j == 0:
                pl.when(b > 0)(go)
            else:
                go()
        return carry

    lax.fori_loop(0, 8, dispatch, 0)
    arr[0] = send[0]

    for copy in w_in:
        copy.wait()

    me_lane = dp * 16 + ex
    lane_io = lax.broadcasted_iota(jnp.int32, (1, 1, 1, 128), 3)
    mix_row = lax.broadcasted_iota(jnp.int32, (GS, 8, 1), 1)

    def experts(g, carry):
        chunk = pl.ds(g * GS, GS)

        def arrived(i, inner):
            @pl.when(i > 0)
            def _():
                meta_copy(i, (0, 0, 0)).wait_recv()
                send_copy(i, (0, 0, 0)).wait_recv()

            return inner

        lax.fori_loop(g * GS, g * GS + GS, arrived, 0)
        mix = pltpu.make_async_remote_copy(
            arr.at[chunk, 1], pmix.at[chunk], mix_s.at[g], mix_r.at[g],
            device_id=partner, device_id_type=MESH,
        )
        mix.start()

        def load_own(n, inner):
            cols = pl.ds(pl.multiple_of(n * CT, CT), CT)
            xs[0 : GS * 16, cols] = arr[chunk, :, :, cols].astype(F32).reshape(GS * 16, CT).astype(BF16)
            return inner

        lax.fori_loop(0, NT, load_own, 0)
        mix.wait()

        def load_mix(n, inner):
            cols = pl.ds(pl.multiple_of(n * CT, CT), CT)
            xs[GS * 16 : GS * 24, cols] = pmix[chunk, :, cols].astype(F32).reshape(GS * 8, CT).astype(BF16)
            return inner

        lax.fori_loop(0, NT, load_mix, 0)

        def hidden(n, inner):
            cols = pl.ds(pl.multiple_of(n * 256, 256), 256)
            gate = jnp.dot(xs[...], wg[:, cols], preferred_element_type=F32)
            up = jnp.dot(xs[...], wu[:, cols], preferred_element_type=F32)
            hid[:, cols] = (gate / (1.0 + jnp.exp(-gate)) * up).astype(BF16)
            return inner

        lax.fori_loop(0, FF // 256, hidden, 0)

        def down(n, inner):
            cols = pl.ds(pl.multiple_of(n * CT, CT), CT)
            rows = jnp.dot(hid[...], wd[:, cols], preferred_element_type=F32)
            arr[chunk, :, :, cols] = rows[0 : GS * 16].reshape(GS, 2, 8, CT).astype(BF16)
            pmix[chunk, :, cols] = rows[GS * 16 :].reshape(GS, 8, CT).astype(BF16)
            return inner

        lax.fori_loop(0, NT, down, 0)
        back = pltpu.make_async_remote_copy(
            pmix.at[chunk], pout.at[chunk], po_s.at[g], po_r.at[g],
            device_id=partner, device_id_type=MESH,
        )
        back.start()
        found = jnp.sum(jnp.where(lane_io == me_lane, meta[chunk], 0.0), axis=3, keepdims=True)
        own0, own1 = found[:, 0], found[:, 1]
        bound = jnp.where(mix_row < 4, own0, own1)
        mine = (4 + lax.rem(mix_row, 4)).astype(F32) < bound
        back.wait()

        def choose(n, inner):
            cols = pl.ds(pl.multiple_of(n * CT, CT), CT)
            own = arr[chunk, 1, :, cols].astype(F32)
            other = pout[chunk, :, cols].astype(F32)
            arr[chunk, 1, :, cols] = jnp.where(mine, own, other).astype(BF16)
            return inner

        lax.fori_loop(0, NT, choose, 0)
        for h in range(GS // 8):
            offs = offsets_of(g * (GS // 8) + h)
            for j in range(8):
                i = g * GS + h * 8 + j

                def go(i=i, o=offs[j]):
                    ret_copy(i, o).start()

                if h == 0 and j == 0:
                    pl.when(g > 0)(go)
                else:
                    go()
        return carry

    lax.fori_loop(0, NG, experts, 0)
    ret[0] = arr[0]
    acc[...] = jnp.zeros_like(acc)

    def combine(g, carry):
        def arrived(i, inner):
            @pl.when(i > 0)
            def _():
                ret_copy(i, (0, 0, 0)).wait_recv()

            return inner

        lax.fori_loop(g * GS, g * GS + GS, arrived, 0)
        blocks = []
        for h in range(GS // 8):
            offs = offsets_of(g * (GS // 8) + h)
            for j in range(8):
                pair = pair_at(offs[j])
                blocks.append(
                    jnp.where(row_io == aux_row(0, pair), aux_row(2, pair), 0.0)
                    + jnp.where(row_io == aux_row(1, pair), aux_row(3, pair), 0.0)
                )
        mixer = jnp.transpose(jnp.concatenate(blocks, axis=0))
        high = mixer.astype(BF16)
        comb[0:256, :] = high
        comb[256:512, :] = (mixer - high.astype(F32)).astype(BF16)

        def tile(n, inner):
            cols = pl.ds(pl.multiple_of(n * CT, CT), CT)
            rows = ret[pl.ds(g * GS, GS), :, :, cols].astype(F32).reshape(GS * 16, CT).astype(BF16)
            both = jnp.dot(comb[...], rows, preferred_element_type=F32)
            acc[:, :, cols] += (both[0:256] + both[256:512]).reshape(2, 128, CT)
            return inner

        lax.fori_loop(0, NT, tile, 0)
        return carry

    lax.fori_loop(0, NG, combine, 0)

    def part_copy(n):
        cols = pl.ds(pl.multiple_of(n * CT, CT), CT)
        return pltpu.make_async_remote_copy(
            acc.at[1 - c, :, cols], part.at[:, cols], part_s.at[n], part_r.at[n],
            device_id=partner, device_id_type=MESH,
        )

    def part_go(n, carry):
        part_copy(n).start()
        return carry

    lax.fori_loop(0, NT, part_go, 0)

    def finish(n, carry):
        cols = pl.ds(pl.multiple_of(n * CT, CT), CT)
        part_copy(n).wait_recv()
        out_ref[:, cols] = (acc[c, :, cols] + part[:, cols]).astype(BF16)
        return carry

    lax.fori_loop(0, NT, finish, 0)

    def drain(i, carry):
        meta_copy(i, (0, 0, 0)).wait_send()
        send_copy(i, (0, 0, 0)).wait_send()
        ret_copy(i, (0, 0, 0)).wait_send()
        return carry

    lax.fori_loop(1, CHIPS, drain, 0)

    def part_drain(n, carry):
        part_copy(n).wait_send()
        return carry

    lax.fori_loop(0, NT, part_drain, 0)


def local(tokens, router_weights, expert_ids, gate_weight, up_weight, down_weight):
    sem = pltpu.SemaphoreType.DMA
    hbm = pl.BlockSpec(memory_space=pl.ANY)
    vmem = pl.BlockSpec(memory_space=pltpu.VMEM)
    return pl.pallas_call(
        kernel,
        out_shape=jax.ShapeDtypeStruct((128, D), BF16),
        in_specs=[hbm, vmem, vmem, hbm, hbm, hbm],
        out_specs=vmem,
        scratch_shapes=[
            pltpu.VMEM((2, 128, D), BF16),
            pltpu.VMEM((2, 4, 64, 128), F32),
            pltpu.VMEM((4, 64, 128), F32),
            pltpu.VMEM((2, 1, 128), F32),
            pltpu.VMEM((CHIPS, 2, 1, 128), F32),
            pltpu.VMEM((128, 256), BF16),
            pltpu.VMEM((CHIPS, 2, 8, D), BF16),
            pltpu.VMEM((CHIPS, 2, 8, D), BF16),
            pltpu.VMEM((CHIPS, 8, D), BF16),
            pltpu.VMEM((CHIPS, 8, D), BF16),
            pltpu.VMEM((CHIPS, 2, 8, D), BF16),
            pltpu.VMEM((D, FF), BF16),
            pltpu.VMEM((D, FF), BF16),
            pltpu.VMEM((FF, D), BF16),
            pltpu.VMEM((GS * 24, D), BF16),
            pltpu.VMEM((GS * 24, FF), BF16),
            pltpu.VMEM((512, GS * 16), BF16),
            pltpu.VMEM((2, 128, D), F32),
            pltpu.VMEM((128, D), F32),
            sem, sem((3,)), sem((3,)), sem((3,)),
            sem((CHIPS,)), sem((CHIPS,)), sem((CHIPS,)), sem((CHIPS,)), sem((CHIPS,)), sem((CHIPS,)),
            sem((NG,)), sem((NG,)), sem((NG,)), sem((NG,)), sem((NT,)), sem((NT,)),
        ],
        compiler_params=pltpu.CompilerParams(
            collective_id=0, has_side_effects=True, vmem_limit_bytes=67043328
        ),
    )(
        tokens, expert_ids.T, router_weights.T,
        gate_weight[0], up_weight[0], down_weight[0],
    )


def solution(mesh):
    split = ("dp", "expert")
    return jax.shard_map(
        local,
        mesh=mesh,
        in_specs=(
            P(split, None), P(split, None), P(split, None),
            P(split, None, None), P(split, None, None), P(split, None, None),
        ),
        out_specs=P(split, None),
        check_vma=False,
    )
```

time: 867 us -> 305 us (0.35)
  the two profiles are of different devices: /device:TPU:5 before, /device:TPU:15 now
where the time goes in v1:
time: 305 us
  Pallas kernels  303 us (99%)
    pallas_call x1, Pallas kernels, local(): pl.pallas_call(kernel, out_shape=jax.ShapeDtypeStruct((128, D), BF16), in...  303 us

profile of v1, /device:TPU:15, one launch (start us, length us, event | category | flops | bytes accessed | tf_op | source)
XLA Modules:
  0.0 304.9 jit_solution(17148502071618190257)
XLA Ops:
  0.0 302.6 %shard_map.64 = bf16[128,4096]{1,0:T(8,128)(2,1)} custom-call(bf16[128,4096]{1,0:T(8,128)(2,1)} %tok_hbm.1, s32[8,128]{1,0:T(8,128)} %bitcast.8, f32[8,128]{1,0:T(8,128)} %bitcast.9, bf16[4096,768]{1,0:T(8,128)(2,1)} %bitcast.5, bf16[4096,768]{1,0:T(8,128)(2,1)} %bitcast.6, bf16[768,4096]{1,0:T(8,128)(2,1)} %bitcast.7), custom_call_target="tpu_custom_call" | custom-call | tf_op jit(solution)/shard_map/pallas_call | solution.py:393
  302.6 2.3 copy.8

commit v2 on v1

--- a/solution.py
+++ b/solution.py
@@ -182,6 +182,22 @@
             device_id=device_at(o, -1), device_id_type=MESH,
         )
 
+    def tell(b, carry):
+        offs = offsets_of(b)
+        for j in range(8):
+            i = b * 8 + j
+
+            def go(i=i, j=j):
+                meta_copy(i, offs[j]).start()
+
+            if j == 0:
+                pl.when(b > 0)(go)
+            else:
+                go()
+        return carry
+
+    lax.fori_loop(0, 8, tell, 0)
+
     row_io = lax.broadcasted_iota(jnp.int32, (16, 256), 0).astype(F32)
 
     def aux_row(k, pair):
@@ -209,7 +225,6 @@
             i = b * 8 + j
 
             def go(i=i, j=j):
-                meta_copy(i, offs[j]).start()
                 send_copy(i, offs[j]).start()
 
             if j == 0:

time: 305 us -> 298 us (0.977)
  Pallas kernels: 303 us -> 293 us
    pallas_call x1, Pallas kernels: 303 us -> 293 us  [local(): pl.pallas_call(kernel, out_shape=jax.ShapeDtypeStruct((128, D), BF16), in...]
where the time goes in v2:
time: 298 us; the launch traced here: 296 us
  Pallas kernels  293 us (98%)
    pallas_call x1, Pallas kernels, local(): pl.pallas_call(kernel, out_shape=jax.ShapeDtypeStruct((128, D), BF16), in...  293 us

profile of v2, /device:TPU:15, one launch (start us, length us, event | category | flops | bytes accessed | tf_op | source)
XLA Modules:
  0.0 295.6 jit_solution(16982421829957152864)
XLA Ops:
  0.0 293.3 %shard_map.64 = bf16[128,4096]{1,0:T(8,128)(2,1)} custom-call(bf16[128,4096]{1,0:T(8,128)(2,1)} %tok_hbm.1, s32[8,128]{1,0:T(8,128)} %bitcast.8, f32[8,128]{1,0:T(8,128)} %bitcast.9, bf16[4096,768]{1,0:T(8,128)(2,1)} %bitcast.5, bf16[4096,768]{1,0:T(8,128)(2,1)} %bitcast.6, bf16[768,4096]{1,0:T(8,128)(2,1)} %bitcast.7), custom_call_target="tpu_custom_call" | custom-call | tf_op jit(solution)/shard_map/pallas_call | solution.py:408
  293.3 2.3 copy.8
